TPU v7x, 256 devices: a whole 4x4x8 slice. The times are simulated.
256 devices in a mesh: gy: 8 (over y_lo, x), gz: 32 (over y_hi, z, core).
Axes of the slice: x: 4, y: 4 (y_hi: 2, y_lo: 2; y = y_hi * 2 + y_lo), z: 8, core: 2. Of those that a mesh axis runs over, the one named last changes fastest.
Arguments:
- velocity_modes: float32 [3, 64, 512, 576], P(None, None, 'gy', 'gz'), may hold values from -0.36 to 0.36
- conformation: float32 [6, 64, 512, 1152], P(None, 'gz', 'gy'), may hold values from -0.5 to 16, as said below
Outputs:
- conformation_next: float32 [6, 64, 512, 1152], P(None, 'gz', 'gy')
- stress_modes: float32 [3, 64, 512, 576], P(None, None, 'gy', 'gz')
Inputs may be any that keep to these rules, and one draw needn't show every extreme that they name: `conformation`: components 0, 3 and 5 (the diagonal) lie in 1 to 16 and the others in -0.5 to 0.5, so the trace is at most 48.
All inputs are finite; a program needn't handle non-finite values.
Results may differ from a plain program's by a relative error of at most 0.0003.
Values sent between devices are 32-bit elements; how exact they have to be, the bound alone decides.
A program may use at most 128 MiB of HBM per device.

v0:
```python
import functools
import math

import jax
import jax.numpy as jnp
import ml_dtypes
import numpy as np
from jax import lax
from jax.experimental import pallas as pl
from jax.experimental.pallas import tpu as pltpu
from jax.sharding import PartitionSpec as P

max_extension = 60.0
time_step = 0.25
relax_time = 4.0
stress_scale = 0.2
component_index = ((0, 1, 2), (1, 3, 4), (2, 4, 5))
MESH = pl.DeviceIdType.MESH
edge = 8


def round_up(value, unit):
    return (value + unit - 1) // unit * unit


@functools.lru_cache
def spanwise_tables(modes, points, depth):
    half = modes // 2
    index_j = np.arange(modes, dtype=np.int64)
    index_n = np.arange(points, dtype=np.int64)
    wave = np.where(index_j < half, index_j, index_j - half + 1)
    theta = (wave[:, None] * index_n[None, :] % points) * (2.0 * math.pi / points)
    rate = wave[:, None] * (2.0 * math.pi / points)
    is_cosine = (index_j < half)[:, None]
    basis = np.where(is_cosine, np.cos(theta), np.sin(theta))
    slope = np.where(is_cosine, -rate * np.sin(theta), rate * np.cos(theta))
    tables = []
    for table in (basis, slope):
        table = np.pad(table, ((0, depth - modes), (0, 0))).astype(np.float32)
        head = table.astype(ml_dtypes.bfloat16)
        rest = (table - head.astype(np.float32)).astype(ml_dtypes.bfloat16)
        tables.append(np.concatenate([head, rest], axis=0))
    return tables


def split(value):
    head = value.astype(jnp.bfloat16)
    return head, (value - head.astype(jnp.float32)).astype(jnp.bfloat16)


def kernel(
    dims,
    vm, conf, tab_b, tab_s,
    out, sout,
    vmv, confx, fac, send, recv, osend, orecv, cols, rows, vhalo, yhalo, lhs, velx, veldz,
    nxt, tbv, tsv, pull, res, sbuf,
    load_sem, tab_sem, own_sem, out_sem,
    a2a_send, a2a_recv, o2a_send, o2a_recv,
    cx_send, cx_recv, cy_send, cy_recv, vx_send, vx_recv, vy_send, vy_recv,
):
    ngy, ngz, nm, ny, nz, depth = dims
    modes = nm * ngz
    gy = lax.axis_index("gy")
    gz = lax.axis_index("gz")
    right = lax.rem(gz + 1, ngz)
    left = lax.rem(gz + ngz - 1, ngz)
    has_low = gy > 0
    has_high = gy < ngy - 1
    body = slice(edge, edge + ny)
    f32 = jnp.float32

    load_vm = pltpu.make_async_copy(vm, vmv, load_sem.at[0])
    load_vm.start()
    load_conf = pltpu.make_async_copy(conf, confx.at[:, 1:3, body, :], load_sem.at[1])
    load_conf.start()
    table_loads = []
    for index, (source, target) in enumerate(((tab_b, tbv), (tab_s, tsv))):
        table_loads.append(
            pltpu.make_async_copy(source, target.at[0 : 2 * depth], tab_sem.at[2 * index])
        )
        table_loads.append(
            pltpu.make_async_copy(
                source.at[0:depth], target.at[2 * depth : 3 * depth], tab_sem.at[2 * index + 1]
            )
        )
    for load in table_loads:
        load.start()

    barrier = pltpu.get_barrier_semaphore()

    def greet(step, carry):
        peer = lax.rem(gz + step, ngz)
        pl.semaphore_signal(barrier, inc=1, device_id=(gy, peer), device_id_type=MESH)
        return carry

    lax.fori_loop(1, ngz, greet, 0)

    @pl.when(has_low)
    def _():
        pl.semaphore_signal(barrier, inc=1, device_id=(gy - 1, gz), device_id_type=MESH)

    @pl.when(has_high)
    def _():
        pl.semaphore_signal(barrier, inc=1, device_id=(gy + 1, gz), device_id_type=MESH)

    low_count = lax.div(gy + ngy - 1, ngy)
    high_count = lax.div(2 * ngy - 2 - gy, ngy)
    pl.semaphore_wait(barrier, ngz - 1 + low_count + high_count)

    cx_up = [
        pltpu.make_async_remote_copy(
            conf.at[c, 1], confx.at[c, 0, body, :], cx_send.at[0, c], cx_recv.at[0, c],
            device_id=(gy, right), device_id_type=MESH,
        )
        for c in range(6)
    ]
    cx_down = [
        pltpu.make_async_remote_copy(
            conf.at[c, 0], confx.at[c, 3, body, :], cx_send.at[1, c], cx_recv.at[1, c],
            device_id=(gy, left), device_id_type=MESH,
        )
        for c in range(6)
    ]
    cy_up = pltpu.make_async_remote_copy(
        conf.at[:, :, ny - edge : ny, :], confx.at[:, 1:3, 0:edge, :],
        cy_send.at[0], cy_recv.at[0], device_id=(gy + 1, gz), device_id_type=MESH,
    )
    cy_down = pltpu.make_async_remote_copy(
        conf.at[:, :, 0:edge, :], confx.at[:, 1:3, edge + ny : ny + 2 * edge, :],
        cy_send.at[1], cy_recv.at[1], device_id=(gy - 1, gz), device_id_type=MESH,
    )
    for c in range(6):
        cx_up[c].start()
        cx_down[c].start()

    @pl.when(has_high)
    def _():
        cy_up.start()

    @pl.when(has_low)
    def _():
        cy_down.start()

    load_vm.wait()

    def pack(cm, carry):
        even = vmv[cm, pl.ds(0, ngz, stride=2), :]
        odd = vmv[cm, pl.ds(1, ngz, stride=2), :]
        send[:, cm, :] = jnp.concatenate([even, odd], axis=1)
        return carry

    lax.fori_loop(0, 3 * nm, pack, 0)

    def message(source, target, send_sem, recv_sem, mine, theirs, peer):
        return pltpu.make_async_remote_copy(
            source.at[mine], target.at[theirs], send_sem.at[mine], recv_sem.at[theirs],
            device_id=(gy, peer), device_id_type=MESH,
        )

    def exchange_start(source, target, send_sem, recv_sem, own):
        def start(step, carry):
            peer = lax.rem(gz + step, ngz)
            message(source, target, send_sem, recv_sem, peer, gz, peer).start()
            return carry

        lax.fori_loop(1, ngz, start, 0)
        pltpu.make_async_copy(source.at[gz], target.at[gz], own).start()

    def exchange_recv(source, target, send_sem, recv_sem, own):
        def wait(step, carry):
            peer = lax.rem(gz + ngz - step, ngz)
            message(source, target, send_sem, recv_sem, peer, peer, peer).wait_recv()
            return carry

        pltpu.make_async_copy(source.at[gz], target.at[gz], own).wait()
        lax.fori_loop(1, ngz, wait, 0)

    def exchange_sent(source, target, send_sem, recv_sem):
        def wait(step, carry):
            peer = lax.rem(gz + step, ngz)
            message(source, target, send_sem, recv_sem, peer, peer, peer).wait_send()
            return carry

        lax.fori_loop(1, ngz, wait, 0)

    exchange_start(send, recv, a2a_send, a2a_recv, own_sem.at[0])

    load_conf.wait()
    for load in table_loads:
        load.wait()
    for c in range(6):
        cx_up[c].wait_recv()
        cx_down[c].wait_recv()

    @pl.when(has_low)
    def _():
        cy_up.wait_recv()

    @pl.when(has_high)
    def _():
        cy_down.wait_recv()

    @pl.when(jnp.logical_not(has_low))
    def _():
        confx[:, 1:3, 0:edge, :] = jnp.zeros((6, 2, edge, nz), f32)

    @pl.when(jnp.logical_not(has_high))
    def _():
        confx[:, 1:3, edge + ny : ny + 2 * edge, :] = jnp.zeros((6, 2, edge, nz), f32)

    def factor_rows(plane, first):
        at = pl.ds(first, 8)
        trace = confx[0, plane, at, :] + confx[3, plane, at, :] + confx[5, plane, at, :]
        fac[plane, at, :] = (max_extension - 3.0) / (max_extension - trace)

    def factor_outer(block, carry):
        first = pl.multiple_of(edge + block * 8, 8)
        factor_rows(0, first)
        factor_rows(3, first)
        return carry

    def factor_inner(block, carry):
        first = pl.multiple_of(block * 8, 8)
        factor_rows(1, first)
        factor_rows(2, first)
        return carry

    lax.fori_loop(0, ny // 8, factor_outer, 0)
    lax.fori_loop(0, ny // 8 + 2, factor_inner, 0)

    weight = 2.0 / nz

    def stress_rows(step, carry):
        plane = step // (ny // 16)
        first = pl.multiple_of(edge + (step % (ny // 16)) * 16, 8)
        here = pl.ds(first, 16)
        around = pl.ds(pl.multiple_of(first - 8, 8), 32)
        for row in range(3):
            cx, cy, cz = component_index[row]
            pulled = fac[plane + 1, around, :] * confx[cy, plane + 1, around, :]
            along = (
                fac[plane + 2, here, :] * confx[cx, plane + 2, here, :]
                - fac[plane, here, :] * confx[cx, plane, here, :]
            ) + (pulled[9:25] - pulled[7:23])
            spanwise = fac[plane + 1, here, :] * confx[cz, plane + 1, here, :]
            at = pl.ds(pl.multiple_of(row * 2 * ny + plane * ny + first - edge, 16), 16)
            head, rest = split(along * (0.5 * stress_scale * weight))
            pull[0, at, :] = head
            pull[1, at, :] = rest
            head, rest = split(spanwise * (-stress_scale * weight))
            pull[2, at, :] = head
            pull[3, at, :] = rest
        return carry

    lax.fori_loop(0, 2 * (ny // 16), stress_rows, 0)

    chunk = modes // 2

    def across(a, b):
        return lax.dot_general(a, b, (((1,), (1,)), ((), ())), preferred_element_type=f32)

    def project(step, carry):
        first = pl.multiple_of(step * chunk, 16)
        head = pl.ds(first, chunk)
        rest = pl.ds(pl.multiple_of(depth + first, 16), chunk)
        total = across(tbv[head, :], pull[0]) + across(tsv[head, :], pull[2])
        total = total + (across(tbv[head, :], pull[1]) + across(tsv[head, :], pull[3]))
        total = total + (across(tbv[rest, :], pull[0]) + across(tsv[rest, :], pull[2]))
        res[pl.ds(first, chunk), :] = total
        return carry

    lax.fori_loop(0, 2, project, 0)
    head_row = lax.broadcasted_iota(jnp.int32, (8, 6 * ny), 0) == 0
    res[0:8, :] = jnp.where(head_row, 0.5 * res[0:8, :], res[0:8, :])
    for k in range(ngz):
        for c in range(3):
            osend[k, c * nm : (c + 1) * nm, :] = res[
                k * nm : (k + 1) * nm, c * 2 * ny : (c + 1) * 2 * ny
            ]
    exchange_start(osend, orecv, o2a_send, o2a_recv, own_sem.at[1])

    exchange_recv(send, recv, a2a_send, a2a_recv, own_sem.at[0])
    for c in range(3):
        cols[c, modes:depth, :] = jnp.zeros((depth - modes, 2 * ny), f32)
        for k in range(ngz):
            cols[c, k * nm : (k + 1) * nm, :] = recv[k, c * nm : (c + 1) * nm, :]
        turned = cols[c].T
        rows[c] = turned.reshape(2, ny, depth)

    vx_up = pltpu.make_async_remote_copy(
        rows.at[:, 1], vhalo.at[0], vx_send.at[0], vx_recv.at[0],
        device_id=(gy, right), device_id_type=MESH,
    )
    vx_down = pltpu.make_async_remote_copy(
        rows.at[:, 0], vhalo.at[1], vx_send.at[1], vx_recv.at[1],
        device_id=(gy, left), device_id_type=MESH,
    )
    vy_up = pltpu.make_async_remote_copy(
        rows.at[:, :, ny - edge : ny, :], yhalo.at[0], vy_send.at[0], vy_recv.at[0],
        device_id=(gy + 1, gz), device_id_type=MESH,
    )
    vy_down = pltpu.make_async_remote_copy(
        rows.at[:, :, 0:edge, :], yhalo.at[1], vy_send.at[1], vy_recv.at[1],
        device_id=(gy - 1, gz), device_id_type=MESH,
    )
    vx_up.start()
    vx_down.start()

    @pl.when(has_high)
    def _():
        vy_up.start()

    @pl.when(has_low)
    def _():
        vy_down.start()

    def put_lhs(first, value):
        head, rest = split(value)
        at = slice(first, first + value.shape[0])
        lhs[at, 0:depth] = head
        lhs[at, depth : 2 * depth] = head
        lhs[at, 2 * depth : 3 * depth] = rest

    for c in range(3):
        for p in range(2):
            put_lhs((c * 2 + p) * ny, rows[c, p])

    wide = nz // 3

    def spread_own(step, carry):
        at = pl.ds(pl.multiple_of(step * wide, 128), wide)
        fine = jnp.dot(lhs[0 : 6 * ny, :], tbv[:, at], preferred_element_type=f32)
        velx[:, 1:3, body, at] = fine.reshape(3, 2, ny, wide)
        fine = jnp.dot(lhs[0 : 6 * ny, :], tsv[:, at], preferred_element_type=f32)
        veldz[:, :, :, at] = fine.reshape(3, 2, ny, wide)
        return carry

    lax.fori_loop(0, 3, spread_own, 0)

    vx_up.wait_recv()
    vx_down.wait_recv()

    @pl.when(has_low)
    def _():
        vy_up.wait_recv()

    @pl.when(has_high)
    def _():
        vy_down.wait_recv()

    @pl.when(jnp.logical_not(has_low))
    def _():
        yhalo[0] = jnp.zeros((3, 2, edge, depth), f32)

    @pl.when(jnp.logical_not(has_high))
    def _():
        yhalo[1] = jnp.zeros((3, 2, edge, depth), f32)

    for side in range(2):
        for c in range(3):
            put_lhs((6 + side * 3 + c) * ny, vhalo[side, c])
        put_lhs(12 * ny + side * 6 * edge, yhalo[side].reshape(6 * edge, depth))

    def spread_halo(step, carry):
        at = pl.ds(pl.multiple_of(step * wide, 128), wide)
        fine = jnp.dot(lhs[6 * ny : 12 * ny + 12 * edge, :], tbv[:, at], preferred_element_type=f32)
        velx[:, 0, body, at] = fine[0 : 3 * ny].reshape(3, ny, wide)
        velx[:, 3, body, at] = fine[3 * ny : 6 * ny].reshape(3, ny, wide)
        low = fine[6 * ny : 6 * ny + 6 * edge].reshape(3, 2, edge, wide)
        high = fine[6 * ny + 6 * edge :].reshape(3, 2, edge, wide)
        velx[:, 1:3, 0:edge, at] = low
        velx[:, 1:3, edge + ny :, at] = high
        return carry

    lax.fori_loop(0, 3, spread_halo, 0)

    quarter = time_step

    def update_rows(step, carry):
        plane = step // (ny // 8)
        first = pl.multiple_of(edge + (step % (ny // 8)) * 8, 8)
        here = pl.ds(first, 8)
        around = pl.ds(pl.multiple_of(first - 8, 8), 24)
        target = pl.ds(pl.multiple_of(first - edge, 8), 8)
        speed = [quarter * velx[a, plane + 1, here, :] for a in range(3)]
        plus = [jnp.maximum(s, 0.0) for s in speed]
        minus = [jnp.maximum(-s, 0.0) for s in speed]
        drain = (jnp.abs(speed[0]) + jnp.abs(speed[1])) + jnp.abs(speed[2])
        keep = (1.0 - drain) - (time_step / relax_time) * fac[plane + 1, here, :]
        centre = [confx[c, plane + 1, here, :] for c in range(6)]
        grown = []
        for a in range(3):
            tall = velx[a, plane + 1, around, :]
            grad = (
                (0.5 * quarter) * (velx[a, plane + 2, here, :] - velx[a, plane, here, :]),
                (0.5 * quarter) * (tall[9:17] - tall[7:15]),
                quarter * veldz[a, plane, target, :],
            )
            grown.append(
                [
                    (grad[0] * centre[component_index[0][b]] + grad[1] * centre[component_index[1][b]])
                    + grad[2] * centre[component_index[2][b]]
                    for b in range(3)
                ]
            )
        for c, (a, b) in enumerate(((0, 0), (0, 1), (0, 2), (1, 1), (1, 2), (2, 2))):
            tall = confx[c, plane + 1, around, :]
            total = grown[a][b] + grown[b][a]
            total = total + keep * centre[c]
            total = total + plus[0] * confx[c, plane, here, :]
            total = total + minus[0] * confx[c, plane + 2, here, :]
            total = total + plus[1] * tall[7:15]
            total = total + minus[1] * tall[9:17]
            total = total + plus[2] * pltpu.roll(centre[c], 1, 1)
            total = total + minus[2] * pltpu.roll(centre[c], nz - 1, 1)
            if a == b:
                total = total + time_step / relax_time
            nxt[c, plane, target, :] = total
        return carry

    lax.fori_loop(0, 2 * (ny // 8), update_rows, 0)
    store_out = pltpu.make_async_copy(nxt, out, out_sem.at[0])
    store_out.start()

    exchange_recv(osend, orecv, o2a_send, o2a_recv, own_sem.at[1])

    def unpack(cm, carry):
        pair = orecv[:, cm, :]
        sbuf[cm, pl.ds(0, ngz, stride=2), :] = pair[:, 0:ny]
        sbuf[cm, pl.ds(1, ngz, stride=2), :] = pair[:, ny : 2 * ny]
        return carry

    lax.fori_loop(0, 3 * nm, unpack, 0)
    store_stress = pltpu.make_async_copy(sbuf, sout, out_sem.at[1])
    store_stress.start()

    exchange_sent(send, recv, a2a_send, a2a_recv)
    exchange_sent(osend, orecv, o2a_send, o2a_recv)
    for c in range(6):
        cx_up[c].wait_send()
        cx_down[c].wait_send()
    vx_up.wait_send()
    vx_down.wait_send()

    @pl.when(has_high)
    def _():
        cy_up.wait_send()
        vy_up.wait_send()

    @pl.when(has_low)
    def _():
        cy_down.wait_send()
        vy_down.wait_send()

    store_out.wait()
    store_stress.wait()


def shards(velocity_modes, conformation):
    ngy = lax.axis_size("gy")
    ngz = lax.axis_size("gz")
    _, planes, ny, nm = velocity_modes.shape
    nz = conformation.shape[3]
    modes = nm * ngz
    depth = round_up(modes, 128)
    tab_b, tab_s = (jnp.asarray(t) for t in spanwise_tables(modes, nz, depth))
    vm = jnp.transpose(velocity_modes, (0, 3, 1, 2)).reshape(3 * nm, planes, ny)
    f32, bf16 = jnp.float32, jnp.bfloat16
    dma = pltpu.SemaphoreType.DMA
    anywhere = pl.BlockSpec(memory_space=pl.ANY)
    out, sout = pl.pallas_call(
        functools.partial(kernel, (ngy, ngz, nm, ny, nz, depth)),
        name="fene_step",
        out_shape=(
            jax.ShapeDtypeStruct(conformation.shape, f32),
            jax.ShapeDtypeStruct(vm.shape, f32),
        ),
        in_specs=[anywhere] * 4,
        out_specs=[anywhere] * 2,
        scratch_shapes=[
            pltpu.VMEM((3 * nm, planes, ny), f32),
            pltpu.VMEM((6, 4, ny + 2 * edge, nz), f32),
            pltpu.VMEM((4, ny + 2 * edge, nz), f32),
            pltpu.VMEM((ngz, 3 * nm, 2 * ny), f32),
            pltpu.VMEM((ngz, 3 * nm, 2 * ny), f32),
            pltpu.VMEM((ngz, 3 * nm, 2 * ny), f32),
            pltpu.VMEM((ngz, 3 * nm, 2 * ny), f32),
            pltpu.VMEM((3, depth, 2 * ny), f32),
            pltpu.VMEM((3, 2, ny, depth), f32),
            pltpu.VMEM((2, 3, ny, depth), f32),
            pltpu.VMEM((2, 3, 2, edge, depth), f32),
            pltpu.VMEM((12 * ny + 12 * edge, 3 * depth), bf16),
            pltpu.VMEM((3, 4, ny + 2 * edge, nz), f32),
            pltpu.VMEM((3, 2, ny, nz), f32),
            pltpu.VMEM((6, 2, ny, nz), f32),
            pltpu.VMEM((3 * depth, nz), bf16),
            pltpu.VMEM((3 * depth, nz), bf16),
            pltpu.VMEM((4, 6 * ny, nz), bf16),
            pltpu.VMEM((modes, 6 * ny), f32),
            pltpu.VMEM((3 * nm, planes, ny), f32),
            dma((2,)), dma((4,)), dma((2,)), dma((2,)),
            dma((ngz,)), dma((ngz,)), dma((ngz,)), dma((ngz,)),
            dma((2, 6)), dma((2, 6)), dma((2,)), dma((2,)),
            dma((2,)), dma((2,)), dma((2,)), dma((2,)),
        ],
        compiler_params=pltpu.CompilerParams(
            collective_id=0, has_side_effects=True, vmem_limit_bytes=60 << 20
        ),
    )(vm, conformation, tab_b, tab_s)
    stress = jnp.transpose(sout.reshape(3, nm, planes, ny), (0, 2, 3, 1))
    return out, stress


def solution(mesh):
    return jax.shard_map(
        shards,
        mesh=mesh,
        in_specs=(P(None, None, "gy", "gz"), P(None, "gz", "gy", None)),
        out_specs=(P(None, "gz", "gy", None), P(None, None, "gy", "gz")),
        check_vma=False,
    )
```

profile of v0, /device:TPU:32, one launch (start us, length us, event | category | flops | bytes accessed | tf_op | source)
XLA Modules:
  0.0 101.9 jit_solution(947601175939216410)
XLA Ops:
  0.6 95.9 %fene_step.1 = (f32[6,2,64,1152]{3,2,1,0:T(8,128)}, f32[54,64,64]{2,1,0:T(8,128)}) custom-call(f32[54,64,64]{2,1,0:T(8,128)} %bitcast.7, f32[6,2,64,1152]{3,2,1,0:T(8,128)} %conf.1, bf16[1280,1152]{1,0:T(8,128)(2,1)} %constant.4.clone.tab_b, bf16[1280,1152]{1,0:T(8,128)(2,1)} %constant.5.clone.tab_s), custom_call_target="tpu_custom_call" | custom-call | tf_op jit(solution)/shard_map/fene_step/pallas_call | solution.py:471
  96.6 0.0 copy-start
  96.6 4.2 %copy.8 = f32[6,2,64,1152]{3,2,1,0:T(8,128)} copy(f32[6,2,64,1152]{3,2,1,0:T(8,128)} %get-tuple-element.8) | data formatting | bytes 7077888
  100.7 0.0 copy-done
  100.7 1.2 %copy.9 = f32[3,64,64,18]{2,1,3,0:T(8,128)} copy(f32[3,64,64,18]{2,1,3,0:T(8,128)S(1)} %bitcast.6) | data formatting | bytes 1769472
Async XLA Ops:
  96.6 4.2 %copy-start = (f32[54,64,64]{2,1,0:T(8,128)S(1)}, f32[54,64,64]{2,1,0:T(8,128)}, u32[]{:S(2)}) copy-start(f32[54,64,64]{2,1,0:T(8,128)} %get-tuple-element.5) | copy-start | bytes 2654212
where the time goes:
time: 103 us; the launch traced here: 102 us
  Pallas kernels  95.9 us (93%)
  local copies, waits for them, and re-layouts  5.36 us (5%)
    pallas_call x1, Pallas kernels, shards(): pl.pallas_call(functools.partial(kernel, (ngy, ngz, nm, ny, nz, depth)),...  95.9 us
    unnamed x4, local copies, waits for them, and re-layouts  5.36 us

commit v1 on v0

--- a/solution.py
+++ b/solution.py
@@ -67,7 +67,9 @@
     has_low = gy > 0
     has_high = gy < ngy - 1
     body = slice(edge, edge + ny)
+    tall = send.shape[0] // ngz
     f32 = jnp.float32
+    pieces = ((0, 2 * nz // 3), (2 * nz // 3, nz // 3))
 
     load_vm = pltpu.make_async_copy(vm, vmv, load_sem.at[0])
     load_vm.start()
@@ -86,6 +88,20 @@
     for load in table_loads:
         load.start()
 
+    ring = ngz // 4
+    core = lax.rem(gz, 2)
+    chip = lax.rem(lax.div(gz, 2), ring)
+    high = lax.div(gz, 2 * ring)
+
+    def peer_of(step, way):
+        turn = lax.div(step, 4)
+        hop = lax.div(turn + 1, 2) * (2 * lax.rem(turn, 2) - 1)
+        return (
+            lax.rem(high + lax.rem(lax.div(step, 2), 2), 2) * (2 * ring)
+            + lax.rem(chip + way * hop + ring, ring) * 2
+            + lax.rem(core + lax.rem(step, 2), 2)
+        )
+
     barrier = pltpu.get_barrier_semaphore()
 
     def greet(step, carry):
@@ -102,6 +118,16 @@
     @pl.when(has_high)
     def _():
         pl.semaphore_signal(barrier, inc=1, device_id=(gy + 1, gz), device_id_type=MESH)
+
+    load_vm.wait()
+
+    def pack(cm, carry):
+        even = vmv[cm, pl.ds(0, ngz, stride=2), :]
+        odd = vmv[cm, pl.ds(1, ngz, stride=2), :]
+        send[pl.ds(cm, ngz, stride=tall), :] = jnp.concatenate([even, odd], axis=1)
+        return carry
+
+    lax.fori_loop(0, 3 * nm, pack, 0, unroll=2)
 
     low_count = lax.div(gy + ngy - 1, ngy)
     high_count = lax.div(2 * ngy - 2 - gy, ngy)
@@ -129,6 +155,45 @@
         conf.at[:, :, 0:edge, :], confx.at[:, 1:3, edge + ny : ny + 2 * edge, :],
         cy_send.at[1], cy_recv.at[1], device_id=(gy - 1, gz), device_id_type=MESH,
     )
+    def words(source, peer):
+        return source.at[pl.ds(pl.multiple_of(peer * tall, 8), 3 * nm), :]
+
+    def message(source, target, send_sem, recv_sem, mine, theirs, peer):
+        return pltpu.make_async_remote_copy(
+            words(source, mine), target.at[theirs], send_sem.at[mine], recv_sem.at[theirs],
+            device_id=(gy, peer), device_id_type=MESH,
+        )
+
+    def exchange_start(source, target, send_sem, recv_sem, own):
+        def start(step, carry):
+            peer = peer_of(step, 1)
+            message(source, target, send_sem, recv_sem, peer, gz, peer).start()
+            return carry
+
+        lax.fori_loop(1, ngz, start, 0)
+        pltpu.make_async_copy(words(source, gz), target.at[gz], own).start()
+
+    def exchange_recv(source, target, send_sem, recv_sem, own, use):
+        pltpu.make_async_copy(words(source, gz), target.at[gz], own).wait()
+        use(gz)
+
+        def wait(step, carry):
+            peer = peer_of(step, -1)
+            message(source, target, send_sem, recv_sem, peer, peer, peer).wait_recv()
+            use(peer)
+            return carry
+
+        lax.fori_loop(1, ngz, wait, 0)
+
+    def exchange_sent(source, target, send_sem, recv_sem):
+        def wait(step, carry):
+            peer = peer_of(step, 1)
+            message(source, target, send_sem, recv_sem, peer, peer, peer).wait_send()
+            return carry
+
+        lax.fori_loop(1, ngz, wait, 0)
+
+    exchange_start(send, recv, a2a_send, a2a_recv, own_sem.at[0])
     for c in range(6):
         cx_up[c].start()
         cx_down[c].start()
@@ -141,56 +206,9 @@
     def _():
         cy_down.start()
 
-    load_vm.wait()
-
-    def pack(cm, carry):
-        even = vmv[cm, pl.ds(0, ngz, stride=2), :]
-        odd = vmv[cm, pl.ds(1, ngz, stride=2), :]
-        send[:, cm, :] = jnp.concatenate([even, odd], axis=1)
-        return carry
-
-    lax.fori_loop(0, 3 * nm, pack, 0)
-
-    def message(source, target, send_sem, recv_sem, mine, theirs, peer):
-        return pltpu.make_async_remote_copy(
-            source.at[mine], target.at[theirs], send_sem.at[mine], recv_sem.at[theirs],
-            device_id=(gy, peer), device_id_type=MESH,
-        )
-
-    def exchange_start(source, target, send_sem, recv_sem, own):
-        def start(step, carry):
-            peer = lax.rem(gz + step, ngz)
-            message(source, target, send_sem, recv_sem, peer, gz, peer).start()
-            return carry
-
-        lax.fori_loop(1, ngz, start, 0)
-        pltpu.make_async_copy(source.at[gz], target.at[gz], own).start()
-
-    def exchange_recv(source, target, send_sem, recv_sem, own):
-        def wait(step, carry):
-            peer = lax.rem(gz + ngz - step, ngz)
-            message(source, target, send_sem, recv_sem, peer, peer, peer).wait_recv()
-            return carry
-
-        pltpu.make_async_copy(source.at[gz], target.at[gz], own).wait()
-        lax.fori_loop(1, ngz, wait, 0)
-
-    def exchange_sent(source, target, send_sem, recv_sem):
-        def wait(step, carry):
-            peer = lax.rem(gz + step, ngz)
-            message(source, target, send_sem, recv_sem, peer, peer, peer).wait_send()
-            return carry
-
-        lax.fori_loop(1, ngz, wait, 0)
-
-    exchange_start(send, recv, a2a_send, a2a_recv, own_sem.at[0])
-
     load_conf.wait()
     for load in table_loads:
         load.wait()
-    for c in range(6):
-        cx_up[c].wait_recv()
-        cx_down[c].wait_recv()
 
     @pl.when(has_low)
     def _():
@@ -208,82 +226,69 @@
     def _():
         confx[:, 1:3, edge + ny : ny + 2 * edge, :] = jnp.zeros((6, 2, edge, nz), f32)
 
-    def factor_rows(plane, first):
-        at = pl.ds(first, 8)
+    def factor_of(plane, at):
         trace = confx[0, plane, at, :] + confx[3, plane, at, :] + confx[5, plane, at, :]
-        fac[plane, at, :] = (max_extension - 3.0) / (max_extension - trace)
-
-    def factor_outer(block, carry):
-        first = pl.multiple_of(edge + block * 8, 8)
-        factor_rows(0, first)
-        factor_rows(3, first)
-        return carry
-
-    def factor_inner(block, carry):
-        first = pl.multiple_of(block * 8, 8)
-        factor_rows(1, first)
-        factor_rows(2, first)
-        return carry
-
-    lax.fori_loop(0, ny // 8, factor_outer, 0)
-    lax.fori_loop(0, ny // 8 + 2, factor_inner, 0)
+        return (max_extension - 3.0) / (max_extension - trace)
+
+    def factor_rows(block, carry):
+        at = pl.ds(pl.multiple_of(block * 8, 8), 8)
+        fac[0, at, :] = factor_of(1, at)
+        fac[1, at, :] = factor_of(2, at)
+        return carry
+
+    lax.fori_loop(0, ny // 8 + 2, factor_rows, 0)
 
     weight = 2.0 / nz
 
-    def stress_rows(step, carry):
-        plane = step // (ny // 16)
-        first = pl.multiple_of(edge + (step % (ny // 16)) * 16, 8)
+    def own_rows(step, carry):
+        first = pl.multiple_of(edge + step * 16, 8)
         here = pl.ds(first, 16)
         around = pl.ds(pl.multiple_of(first - 8, 8), 32)
-        for row in range(3):
-            cx, cy, cz = component_index[row]
-            pulled = fac[plane + 1, around, :] * confx[cy, plane + 1, around, :]
-            along = (
-                fac[plane + 2, here, :] * confx[cx, plane + 2, here, :]
-                - fac[plane, here, :] * confx[cx, plane, here, :]
-            ) + (pulled[9:25] - pulled[7:23])
-            spanwise = fac[plane + 1, here, :] * confx[cz, plane + 1, here, :]
-            at = pl.ds(pl.multiple_of(row * 2 * ny + plane * ny + first - edge, 16), 16)
-            head, rest = split(along * (0.5 * stress_scale * weight))
-            pull[0, at, :] = head
-            pull[1, at, :] = rest
-            head, rest = split(spanwise * (-stress_scale * weight))
-            pull[2, at, :] = head
-            pull[3, at, :] = rest
-        return carry
-
-    lax.fori_loop(0, 2 * (ny // 16), stress_rows, 0)
+        target = pl.ds(pl.multiple_of(step * 16, 16), 16)
+        for plane in range(2):
+            for row in range(3):
+                cx, cy, cz = component_index[row]
+                pulled = fac[plane, around, :] * confx[cy, plane + 1, around, :]
+                other = fac[1 - plane, here, :] * confx[cx, 2 - plane, here, :]
+                along = pulled[9:25] - pulled[7:23]
+                nxt[row, plane, target, :] = along + other if plane == 0 else along - other
+                spanwise = fac[plane, here, :] * confx[cz, plane + 1, here, :]
+                at = pl.ds(pl.multiple_of((row * 2 + plane) * ny + step * 16, 16), 16)
+                head, rest = split(spanwise * (-stress_scale * weight))
+                pull[2, at, :] = head
+                pull[3, at, :] = rest
+        return carry
+
+    lax.fori_loop(0, ny // 16, own_rows, 0)
 
     chunk = modes // 2
 
     def across(a, b):
         return lax.dot_general(a, b, (((1,), (1,)), ((), ())), preferred_element_type=f32)
 
-    def project(step, carry):
+    def project(table, which, step):
         first = pl.multiple_of(step * chunk, 16)
-        head = pl.ds(first, chunk)
-        rest = pl.ds(pl.multiple_of(depth + first, 16), chunk)
-        total = across(tbv[head, :], pull[0]) + across(tsv[head, :], pull[2])
-        total = total + (across(tbv[head, :], pull[1]) + across(tsv[head, :], pull[3]))
-        total = total + (across(tbv[rest, :], pull[0]) + across(tsv[rest, :], pull[2]))
-        res[pl.ds(first, chunk), :] = total
-        return carry
-
-    lax.fori_loop(0, 2, project, 0)
-    head_row = lax.broadcasted_iota(jnp.int32, (8, 6 * ny), 0) == 0
-    res[0:8, :] = jnp.where(head_row, 0.5 * res[0:8, :], res[0:8, :])
-    for k in range(ngz):
-        for c in range(3):
-            osend[k, c * nm : (c + 1) * nm, :] = res[
-                k * nm : (k + 1) * nm, c * 2 * ny : (c + 1) * 2 * ny
-            ]
-    exchange_start(osend, orecv, o2a_send, o2a_recv, own_sem.at[1])
-
-    exchange_recv(send, recv, a2a_send, a2a_recv, own_sem.at[0])
+        head = table[pl.ds(first, chunk), :]
+        rest = table[pl.ds(pl.multiple_of(depth + first, 16), chunk), :]
+        total = across(head, pull[which]) + across(head, pull[which + 1])
+        return total + across(rest, pull[which]), pl.ds(first, chunk)
+
+    def project_spanwise(step, carry):
+        total, at = project(tsv, 2, step)
+        res[at, :] = total
+        return carry
+
+    lax.fori_loop(0, 2, project_spanwise, 0)
+
     for c in range(3):
         cols[c, modes:depth, :] = jnp.zeros((depth - modes, 2 * ny), f32)
-        for k in range(ngz):
-            cols[c, k * nm : (k + 1) * nm, :] = recv[k, c * nm : (c + 1) * nm, :]
+
+    def place(k):
+        for c in range(3):
+            cols[c, pl.ds(k * nm, nm), :] = recv[k, c * nm : (c + 1) * nm, :]
+
+    exchange_recv(send, recv, a2a_send, a2a_recv, own_sem.at[0], place)
+    for c in range(3):
         turned = cols[c].T
         rows[c] = turned.reshape(2, ny, depth)
 
@@ -325,17 +330,48 @@
         for p in range(2):
             put_lhs((c * 2 + p) * ny, rows[c, p])
 
-    wide = nz // 3
-
-    def spread_own(step, carry):
-        at = pl.ds(pl.multiple_of(step * wide, 128), wide)
+    for c in range(6):
+        cx_up[c].wait_recv()
+        cx_down[c].wait_recv()
+
+    def halo_rows(step, carry):
+        here = pl.ds(pl.multiple_of(edge + step * 16, 8), 16)
+        target = pl.ds(pl.multiple_of(step * 16, 16), 16)
+        for plane in range(2):
+            outer = factor_of(3 * plane, here)
+            for row in range(3):
+                pulled = outer * confx[component_index[row][0], 3 * plane, here, :]
+                along = nxt[row, plane, target, :]
+                along = along - pulled if plane == 0 else along + pulled
+                at = pl.ds(pl.multiple_of((row * 2 + plane) * ny + step * 16, 16), 16)
+                head, rest = split(along * (0.5 * stress_scale * weight))
+                pull[0, at, :] = head
+                pull[1, at, :] = rest
+        return carry
+
+    lax.fori_loop(0, ny // 16, halo_rows, 0)
+
+    def project_along(step, carry):
+        total, at = project(tbv, 0, step)
+        res[at, :] = res[at, :] + total
+        return carry
+
+    lax.fori_loop(0, 2, project_along, 0)
+    head_row = lax.broadcasted_iota(jnp.int32, (8, 6 * ny), 0) == 0
+    res[0:8, :] = jnp.where(head_row, 0.5 * res[0:8, :], res[0:8, :])
+    for k in range(ngz):
+        for c in range(3):
+            osend[k * tall + c * nm : k * tall + (c + 1) * nm, :] = res[
+                k * nm : (k + 1) * nm, c * 2 * ny : (c + 1) * 2 * ny
+            ]
+    exchange_start(osend, orecv, o2a_send, o2a_recv, own_sem.at[1])
+
+    for first, wide in pieces:
+        at = slice(first, first + wide)
         fine = jnp.dot(lhs[0 : 6 * ny, :], tbv[:, at], preferred_element_type=f32)
         velx[:, 1:3, body, at] = fine.reshape(3, 2, ny, wide)
         fine = jnp.dot(lhs[0 : 6 * ny, :], tsv[:, at], preferred_element_type=f32)
         veldz[:, :, :, at] = fine.reshape(3, 2, ny, wide)
-        return carry
-
-    lax.fori_loop(0, 3, spread_own, 0)
 
     vx_up.wait_recv()
     vx_down.wait_recv()
@@ -361,18 +397,14 @@
             put_lhs((6 + side * 3 + c) * ny, vhalo[side, c])
         put_lhs(12 * ny + side * 6 * edge, yhalo[side].reshape(6 * edge, depth))
 
-    def spread_halo(step, carry):
-        at = pl.ds(pl.multiple_of(step * wide, 128), wide)
+    for first, wide in pieces:
+        at = slice(first, first + wide)
         fine = jnp.dot(lhs[6 * ny : 12 * ny + 12 * edge, :], tbv[:, at], preferred_element_type=f32)
         velx[:, 0, body, at] = fine[0 : 3 * ny].reshape(3, ny, wide)
         velx[:, 3, body, at] = fine[3 * ny : 6 * ny].reshape(3, ny, wide)
         low = fine[6 * ny : 6 * ny + 6 * edge].reshape(3, 2, edge, wide)
-        high = fine[6 * ny + 6 * edge :].reshape(3, 2, edge, wide)
         velx[:, 1:3, 0:edge, at] = low
-        velx[:, 1:3, edge + ny :, at] = high
-        return carry
-
-    lax.fori_loop(0, 3, spread_halo, 0)
+        velx[:, 1:3, edge + ny :, at] = fine[6 * ny + 6 * edge :].reshape(3, 2, edge, wide)
 
     quarter = time_step
 
@@ -386,7 +418,7 @@
         plus = [jnp.maximum(s, 0.0) for s in speed]
         minus = [jnp.maximum(-s, 0.0) for s in speed]
         drain = (jnp.abs(speed[0]) + jnp.abs(speed[1])) + jnp.abs(speed[2])
-        keep = (1.0 - drain) - (time_step / relax_time) * fac[plane + 1, here, :]
+        keep = (1.0 - drain) - (time_step / relax_time) * fac[plane, here, :]
         centre = [confx[c, plane + 1, here, :] for c in range(6)]
         grown = []
         for a in range(3):
@@ -422,15 +454,12 @@
     store_out = pltpu.make_async_copy(nxt, out, out_sem.at[0])
     store_out.start()
 
-    exchange_recv(osend, orecv, o2a_send, o2a_recv, own_sem.at[1])
-
-    def unpack(cm, carry):
-        pair = orecv[:, cm, :]
-        sbuf[cm, pl.ds(0, ngz, stride=2), :] = pair[:, 0:ny]
-        sbuf[cm, pl.ds(1, ngz, stride=2), :] = pair[:, ny : 2 * ny]
-        return carry
-
-    lax.fori_loop(0, 3 * nm, unpack, 0)
+    def unpack(k):
+        pair = orecv[k]
+        sbuf[pl.ds(2 * k, 3 * nm, stride=2 * ngz), :] = pair[:, 0:ny]
+        sbuf[pl.ds(2 * k + 1, 3 * nm, stride=2 * ngz), :] = pair[:, ny : 2 * ny]
+
+    exchange_recv(osend, orecv, o2a_send, o2a_recv, own_sem.at[1], unpack)
     store_stress = pltpu.make_async_copy(sbuf, sout, out_sem.at[1])
     store_stress.start()
 
@@ -473,17 +502,17 @@
         name="fene_step",
         out_shape=(
             jax.ShapeDtypeStruct(conformation.shape, f32),
-            jax.ShapeDtypeStruct(vm.shape, f32),
+            jax.ShapeDtypeStruct((3 * nm * planes, ny), f32),
         ),
         in_specs=[anywhere] * 4,
         out_specs=[anywhere] * 2,
         scratch_shapes=[
             pltpu.VMEM((3 * nm, planes, ny), f32),
             pltpu.VMEM((6, 4, ny + 2 * edge, nz), f32),
-            pltpu.VMEM((4, ny + 2 * edge, nz), f32),
+            pltpu.VMEM((2, ny + 2 * edge, nz), f32),
+            pltpu.VMEM((ngz * round_up(3 * nm, 8), 2 * ny), f32),
             pltpu.VMEM((ngz, 3 * nm, 2 * ny), f32),
-            pltpu.VMEM((ngz, 3 * nm, 2 * ny), f32),
-            pltpu.VMEM((ngz, 3 * nm, 2 * ny), f32),
+            pltpu.VMEM((ngz * round_up(3 * nm, 8), 2 * ny), f32),
             pltpu.VMEM((ngz, 3 * nm, 2 * ny), f32),
             pltpu.VMEM((3, depth, 2 * ny), f32),
             pltpu.VMEM((3, 2, ny, depth), f32),
@@ -497,7 +526,7 @@
             pltpu.VMEM((3 * depth, nz), bf16),
             pltpu.VMEM((4, 6 * ny, nz), bf16),
             pltpu.VMEM((modes, 6 * ny), f32),
-            pltpu.VMEM((3 * nm, planes, ny), f32),
+            pltpu.VMEM((3 * nm * planes, ny), f32),
             dma((2,)), dma((4,)), dma((2,)), dma((2,)),
             dma((ngz,)), dma((ngz,)), dma((ngz,)), dma((ngz,)),
             dma((2, 6)), dma((2, 6)), dma((2,)), dma((2,)),

time: 103 us -> 87.4 us (0.85)
  Pallas kernels: 95.9 us -> 81.4 us
    pallas_call x1, Pallas kernels: 95.9 us -> 81.4 us  [shards(): pl.pallas_call(functools.partial(kernel, (ngy, ngz, nm, ny, nz, depth)),...]
where the time goes in v1:
time: 87.4 us
  Pallas kernels  81.4 us (93%)
  local copies, waits for them, and re-layouts  5.36 us (6%)
    pallas_call x1, Pallas kernels, shards(): pl.pallas_call(functools.partial(kernel, (ngy, ngz, nm, ny, nz, depth)),...  81.4 us
    unnamed x4, local copies, waits for them, and re-layouts  5.36 us

profile of v1, /device:TPU:32, one launch (start us, length us, event | category | flops | bytes accessed | tf_op | source)
XLA Modules:
  0.0 87.4 jit_solution(1034134313149262782)
XLA Ops:
  0.6 81.4 %fene_step.1 = (f32[6,2,64,1152]{3,2,1,0:T(8,128)}, f32[3456,64]{1,0:T(8,128)}) custom-call(f32[54,64,64]{2,1,0:T(8,128)} %bitcast.7, f32[6,2,64,1152]{3,2,1,0:T(8,128)} %conf.1, bf16[1280,1152]{1,0:T(8,128)(2,1)} %constant.4.clone.tab_b, bf16[1280,1152]{1,0:T(8,128)(2,1)} %constant.5.clone.tab_s), custom_call_target="tpu_custom_call" | custom-call | tf_op jit(solution)/shard_map/fene_step/pallas_call | solution.py:500
  82.0 0.0 copy-start
  82.0 4.2 %copy.8 = f32[6,2,64,1152]{3,2,1,0:T(8,128)} copy(f32[6,2,64,1152]{3,2,1,0:T(8,128)} %get-tuple-element.8) | data formatting | bytes 7077888
  86.2 0.0 copy-done
  86.2 1.2 %copy.9 = f32[3,64,64,18]{2,1,3,0:T(8,128)} copy(f32[3,64,64,18]{2,1,3,0:T(8,128)S(1)} %bitcast.6) | data formatting | bytes 1769472
Async XLA Ops:
  82.0 4.2 %copy-start = (f32[3456,64]{1,0:T(8,128)S(1)}, f32[3456,64]{1,0:T(8,128)}, u32[]{:S(2)}) copy-start(f32[3456,64]{1,0:T(8,128)} %get-tuple-element.5) | copy-start | bytes 2654212

commit v2 on v1

--- a/solution.py
+++ b/solution.py
@@ -51,10 +51,10 @@
 def kernel(
     dims,
     vm, conf, tab_b, tab_s,
-    out, sout,
-    vmv, confx, fac, send, recv, osend, orecv, cols, rows, vhalo, yhalo, lhs, velx, veldz,
-    nxt, tbv, tsv, pull, res, sbuf,
-    load_sem, tab_sem, own_sem, out_sem,
+    nxt, sbuf,
+    vmv, confx, fac, send, recv, osend, orecv, cols, rows, vhalo, yhalo, vedge, cedge, cnear, lhs, velx, veldz,
+    tbv, tsv, pull, res,
+    load_sem, tab_sem, own_sem,
     a2a_send, a2a_recv, o2a_send, o2a_recv,
     cx_send, cx_recv, cy_send, cy_recv, vx_send, vx_recv, vy_send, vy_recv,
 ):
@@ -148,11 +148,11 @@
         for c in range(6)
     ]
     cy_up = pltpu.make_async_remote_copy(
-        conf.at[:, :, ny - edge : ny, :], confx.at[:, 1:3, 0:edge, :],
+        cedge.at[1], cnear.at[0],
         cy_send.at[0], cy_recv.at[0], device_id=(gy + 1, gz), device_id_type=MESH,
     )
     cy_down = pltpu.make_async_remote_copy(
-        conf.at[:, :, 0:edge, :], confx.at[:, 1:3, edge + ny : ny + 2 * edge, :],
+        cedge.at[0], cnear.at[1],
         cy_send.at[1], cy_recv.at[1], device_id=(gy - 1, gz), device_id_type=MESH,
     )
     def words(source, peer):
@@ -194,10 +194,18 @@
         lax.fori_loop(1, ngz, wait, 0)
 
     exchange_start(send, recv, a2a_send, a2a_recv, own_sem.at[0])
-    for c in range(6):
+    for c in (0, 3, 5, 1, 2):
         cx_up[c].start()
         cx_down[c].start()
 
+    load_conf.wait()
+    cedge[...] = jnp.zeros_like(cedge)
+    for c in range(6):
+        for p in range(2):
+            at = slice(2 * c + p, 2 * c + p + 1)
+            cedge[0, at, :] = confx[c, 1 + p, edge : edge + 1, :]
+            cedge[1, at, :] = confx[c, 1 + p, edge + ny - 1 : edge + ny, :]
+
     @pl.when(has_high)
     def _():
         cy_up.start()
@@ -206,7 +214,6 @@
     def _():
         cy_down.start()
 
-    load_conf.wait()
     for load in table_loads:
         load.wait()
 
@@ -220,11 +227,18 @@
 
     @pl.when(jnp.logical_not(has_low))
     def _():
-        confx[:, 1:3, 0:edge, :] = jnp.zeros((6, 2, edge, nz), f32)
+        cnear[0] = jnp.zeros((16, nz), f32)
 
     @pl.when(jnp.logical_not(has_high))
     def _():
-        confx[:, 1:3, edge + ny : ny + 2 * edge, :] = jnp.zeros((6, 2, edge, nz), f32)
+        cnear[1] = jnp.zeros((16, nz), f32)
+
+    blank = jnp.zeros((edge - 1, nz), f32)
+    for c in range(6):
+        for p in range(2):
+            at = slice(2 * c + p, 2 * c + p + 1)
+            confx[c, 1 + p, 0:edge, :] = jnp.concatenate([blank, cnear[0, at, :]], axis=0)
+            confx[c, 1 + p, edge + ny :, :] = jnp.concatenate([cnear[1, at, :], blank], axis=0)
 
     def factor_of(plane, at):
         trace = confx[0, plane, at, :] + confx[3, plane, at, :] + confx[5, plane, at, :]
@@ -301,15 +315,24 @@
         device_id=(gy, left), device_id_type=MESH,
     )
     vy_up = pltpu.make_async_remote_copy(
-        rows.at[:, :, ny - edge : ny, :], yhalo.at[0], vy_send.at[0], vy_recv.at[0],
+        vedge.at[1], yhalo.at[0], vy_send.at[0], vy_recv.at[0],
         device_id=(gy + 1, gz), device_id_type=MESH,
     )
     vy_down = pltpu.make_async_remote_copy(
-        rows.at[:, :, 0:edge, :], yhalo.at[1], vy_send.at[1], vy_recv.at[1],
+        vedge.at[0], yhalo.at[1], vy_send.at[1], vy_recv.at[1],
         device_id=(gy - 1, gz), device_id_type=MESH,
     )
     vx_up.start()
     vx_down.start()
+    cx_up[4].start()
+    cx_down[4].start()
+
+    vedge[...] = jnp.zeros_like(vedge)
+    for c in range(3):
+        for p in range(2):
+            at = slice(2 * c + p, 2 * c + p + 1)
+            vedge[0, at, :] = rows[c, p, 0:1, :]
+            vedge[1, at, :] = rows[c, p, ny - 1 : ny, :]
 
     @pl.when(has_high)
     def _():
@@ -330,7 +353,7 @@
         for p in range(2):
             put_lhs((c * 2 + p) * ny, rows[c, p])
 
-    for c in range(6):
+    for c in (0, 3, 5, 1, 2):
         cx_up[c].wait_recv()
         cx_down[c].wait_recv()
 
@@ -386,25 +409,27 @@
 
     @pl.when(jnp.logical_not(has_low))
     def _():
-        yhalo[0] = jnp.zeros((3, 2, edge, depth), f32)
+        yhalo[0] = jnp.zeros((edge, depth), f32)
 
     @pl.when(jnp.logical_not(has_high))
     def _():
-        yhalo[1] = jnp.zeros((3, 2, edge, depth), f32)
-
+        yhalo[1] = jnp.zeros((edge, depth), f32)
+
+    put_lhs(12 * ny, yhalo[...].reshape(2 * edge, depth))
     for side in range(2):
         for c in range(3):
             put_lhs((6 + side * 3 + c) * ny, vhalo[side, c])
-        put_lhs(12 * ny + side * 6 * edge, yhalo[side].reshape(6 * edge, depth))
 
     for first, wide in pieces:
         at = slice(first, first + wide)
-        fine = jnp.dot(lhs[6 * ny : 12 * ny + 12 * edge, :], tbv[:, at], preferred_element_type=f32)
+        fine = jnp.dot(lhs[6 * ny : 12 * ny + 2 * edge, :], tbv[:, at], preferred_element_type=f32)
         velx[:, 0, body, at] = fine[0 : 3 * ny].reshape(3, ny, wide)
         velx[:, 3, body, at] = fine[3 * ny : 6 * ny].reshape(3, ny, wide)
-        low = fine[6 * ny : 6 * ny + 6 * edge].reshape(3, 2, edge, wide)
-        velx[:, 1:3, 0:edge, at] = low
-        velx[:, 1:3, edge + ny :, at] = fine[6 * ny + 6 * edge :].reshape(3, 2, edge, wide)
+        for c in range(3):
+            for p in range(2):
+                row = 6 * ny + 2 * c + p
+                velx[c, 1 + p, edge - 1 : edge, at] = fine[row : row + 1]
+                velx[c, 1 + p, edge + ny : edge + ny + 1, at] = fine[row + edge : row + edge + 1]
 
     quarter = time_step
 
@@ -450,9 +475,9 @@
             nxt[c, plane, target, :] = total
         return carry
 
+    cx_up[4].wait_recv()
+    cx_down[4].wait_recv()
     lax.fori_loop(0, 2 * (ny // 8), update_rows, 0)
-    store_out = pltpu.make_async_copy(nxt, out, out_sem.at[0])
-    store_out.start()
 
     def unpack(k):
         pair = orecv[k]
@@ -460,8 +485,6 @@
         sbuf[pl.ds(2 * k + 1, 3 * nm, stride=2 * ngz), :] = pair[:, ny : 2 * ny]
 
     exchange_recv(osend, orecv, o2a_send, o2a_recv, own_sem.at[1], unpack)
-    store_stress = pltpu.make_async_copy(sbuf, sout, out_sem.at[1])
-    store_stress.start()
 
     exchange_sent(send, recv, a2a_send, a2a_recv)
     exchange_sent(osend, orecv, o2a_send, o2a_recv)
@@ -480,9 +503,6 @@
     def _():
         cy_down.wait_send()
         vy_down.wait_send()
-
-    store_out.wait()
-    store_stress.wait()
 
 
 def shards(velocity_modes, conformation):
@@ -501,11 +521,11 @@
         functools.partial(kernel, (ngy, ngz, nm, ny, nz, depth)),
         name="fene_step",
         out_shape=(
-            jax.ShapeDtypeStruct(conformation.shape, f32),
-            jax.ShapeDtypeStruct((3 * nm * planes, ny), f32),
+            pltpu.VMEM(conformation.shape, f32),
+            pltpu.VMEM((3 * nm * planes, ny), f32),
         ),
         in_specs=[anywhere] * 4,
-        out_specs=[anywhere] * 2,
+        out_specs=[pl.BlockSpec(memory_space=pltpu.VMEM)] * 2,
         scratch_shapes=[
             pltpu.VMEM((3 * nm, planes, ny), f32),
             pltpu.VMEM((6, 4, ny + 2 * edge, nz), f32),
@@ -517,23 +537,24 @@
             pltpu.VMEM((3, depth, 2 * ny), f32),
             pltpu.VMEM((3, 2, ny, depth), f32),
             pltpu.VMEM((2, 3, ny, depth), f32),
-            pltpu.VMEM((2, 3, 2, edge, depth), f32),
-            pltpu.VMEM((12 * ny + 12 * edge, 3 * depth), bf16),
+            pltpu.VMEM((2, edge, depth), f32),
+            pltpu.VMEM((2, edge, depth), f32),
+            pltpu.VMEM((2, 16, nz), f32),
+            pltpu.VMEM((2, 16, nz), f32),
+            pltpu.VMEM((12 * ny + 2 * edge, 3 * depth), bf16),
             pltpu.VMEM((3, 4, ny + 2 * edge, nz), f32),
             pltpu.VMEM((3, 2, ny, nz), f32),
-            pltpu.VMEM((6, 2, ny, nz), f32),
             pltpu.VMEM((3 * depth, nz), bf16),
             pltpu.VMEM((3 * depth, nz), bf16),
             pltpu.VMEM((4, 6 * ny, nz), bf16),
             pltpu.VMEM((modes, 6 * ny), f32),
-            pltpu.VMEM((3 * nm * planes, ny), f32),
-            dma((2,)), dma((4,)), dma((2,)), dma((2,)),
+            dma((2,)), dma((4,)), dma((2,)),
             dma((ngz,)), dma((ngz,)), dma((ngz,)), dma((ngz,)),
             dma((2, 6)), dma((2, 6)), dma((2,)), dma((2,)),
             dma((2,)), dma((2,)), dma((2,)), dma((2,)),
         ],
         compiler_params=pltpu.CompilerParams(
-            collective_id=0, has_side_effects=True, vmem_limit_bytes=60 << 20
+            collective_id=0, has_side_effects=True, vmem_limit_bytes=52 << 20
         ),
     )(vm, conformation, tab_b, tab_s)
     stress = jnp.transpose(sout.reshape(3, nm, planes, ny), (0, 2, 3, 1))

time: 87.4 us -> 82.4 us (0.943)
  Pallas kernels: 81.4 us -> 78.5 us
  local copies, waits for them, and re-layouts: 5.36 us -> 3 us
    pallas_call x1, Pallas kernels: 81.4 us -> 78.5 us  [shards(): pl.pallas_call(functools.partial(kernel, (ngy, ngz, nm, ny, nz, depth)),...]
    unnamed x4 -> x2, local copies, waits for them, and re-layouts: 5.36 us -> 3 us
where the time goes in v2:
time: 82.4 us; the launch traced here: 82.1 us
  Pallas kernels  78.5 us (95%)
  local copies, waits for them, and re-layouts  3 us (4%)
    pallas_call x1, Pallas kernels, shards(): pl.pallas_call(functools.partial(kernel, (ngy, ngz, nm, ny, nz, depth)),...  78.5 us
    unnamed x2, local copies, waits for them, and re-layouts  3 us

profile of v2, /device:TPU:32, one launch (start us, length us, event | category | flops | bytes accessed | tf_op | source)
XLA Modules:
  0.0 82.1 jit_solution(1991526531921247681)
XLA Ops:
  0.6 78.5 %fene_step.1 = (f32[6,2,64,1152]{3,2,1,0:T(8,128)S(1)}, f32[3456,64]{1,0:T(8,128)S(1)}) custom-call(f32[54,64,64]{2,1,0:T(8,128)} %bitcast.7, f32[6,2,64,1152]{3,2,1,0:T(8,128)} %conf.1, bf16[1280,1152]{1,0:T(8,128)(2,1)} %constant.4.clone.tab_b, bf16[1280,1152]{1,0:T(8,128)(2,1)} %constant.5.clone.tab_s), custom_call_target="tpu_custom_call" | custom-call | tf_op jit(solution)/shard_map/fene_step/pallas_call | solution.py:520
  79.1 1.8 %copy.8 = f32[6,2,64,1152]{3,2,1,0:T(8,128)} copy(f32[6,2,64,1152]{3,2,1,0:T(8,128)S(1)} %get-tuple-element.6) | data formatting | bytes 7077888
  80.9 1.2 %copy.9 = f32[3,64,64,18]{2,1,3,0:T(8,128)} copy(f32[3,64,64,18]{2,1,3,0:T(8,128)S(1)} %bitcast.6) | data formatting | bytes 1769472

commit v3 on v2

--- a/solution.py
+++ b/solution.py
@@ -71,6 +71,37 @@
     f32 = jnp.float32
     pieces = ((0, 2 * nz // 3), (2 * nz // 3, nz // 3))
 
+    ring = ngz // 4
+    core = lax.rem(gz, 2)
+    chip = lax.rem(lax.div(gz, 2), ring)
+    high = lax.div(gz, 2 * ring)
+
+    def peer_of(step, way):
+        turn = lax.div(step, 4)
+        hop = lax.div(turn + 1, 2) * (2 * lax.rem(turn, 2) - 1)
+        return (
+            lax.rem(high + lax.rem(lax.div(step, 2), 2), 2) * (2 * ring)
+            + lax.rem(chip + way * hop + ring, ring) * 2
+            + lax.rem(core + lax.rem(step, 2), 2)
+        )
+
+    barrier = pltpu.get_barrier_semaphore()
+
+    def greet(step, carry):
+        peer = lax.rem(gz + step, ngz)
+        pl.semaphore_signal(barrier, inc=1, device_id=(gy, peer), device_id_type=MESH)
+        return carry
+
+    lax.fori_loop(1, ngz, greet, 0)
+
+    @pl.when(has_low)
+    def _():
+        pl.semaphore_signal(barrier, inc=1, device_id=(gy - 1, gz), device_id_type=MESH)
+
+    @pl.when(has_high)
+    def _():
+        pl.semaphore_signal(barrier, inc=1, device_id=(gy + 1, gz), device_id_type=MESH)
+
     load_vm = pltpu.make_async_copy(vm, vmv, load_sem.at[0])
     load_vm.start()
     load_conf = pltpu.make_async_copy(conf, confx.at[:, 1:3, body, :], load_sem.at[1])
@@ -88,37 +119,6 @@
     for load in table_loads:
         load.start()
 
-    ring = ngz // 4
-    core = lax.rem(gz, 2)
-    chip = lax.rem(lax.div(gz, 2), ring)
-    high = lax.div(gz, 2 * ring)
-
-    def peer_of(step, way):
-        turn = lax.div(step, 4)
-        hop = lax.div(turn + 1, 2) * (2 * lax.rem(turn, 2) - 1)
-        return (
-            lax.rem(high + lax.rem(lax.div(step, 2), 2), 2) * (2 * ring)
-            + lax.rem(chip + way * hop + ring, ring) * 2
-            + lax.rem(core + lax.rem(step, 2), 2)
-        )
-
-    barrier = pltpu.get_barrier_semaphore()
-
-    def greet(step, carry):
-        peer = lax.rem(gz + step, ngz)
-        pl.semaphore_signal(barrier, inc=1, device_id=(gy, peer), device_id_type=MESH)
-        return carry
-
-    lax.fori_loop(1, ngz, greet, 0)
-
-    @pl.when(has_low)
-    def _():
-        pl.semaphore_signal(barrier, inc=1, device_id=(gy - 1, gz), device_id_type=MESH)
-
-    @pl.when(has_high)
-    def _():
-        pl.semaphore_signal(barrier, inc=1, device_id=(gy + 1, gz), device_id_type=MESH)
-
     load_vm.wait()
 
     def pack(cm, carry):
@@ -127,7 +127,7 @@
         send[pl.ds(cm, ngz, stride=tall), :] = jnp.concatenate([even, odd], axis=1)
         return carry
 
-    lax.fori_loop(0, 3 * nm, pack, 0, unroll=2)
+    lax.fori_loop(0, 3 * nm, pack, 0, unroll=9)
 
     low_count = lax.div(gy + ngy - 1, ngy)
     high_count = lax.div(2 * ngy - 2 - gy, ngy)
@@ -353,6 +353,13 @@
         for p in range(2):
             put_lhs((c * 2 + p) * ny, rows[c, p])
 
+    for first, wide in pieces:
+        at = slice(first, first + wide)
+        fine = jnp.dot(lhs[0 : 6 * ny, :], tbv[:, at], preferred_element_type=f32)
+        velx[:, 1:3, body, at] = fine.reshape(3, 2, ny, wide)
+        fine = jnp.dot(lhs[0 : 6 * ny, :], tsv[:, at], preferred_element_type=f32)
+        veldz[:, :, :, at] = fine.reshape(3, 2, ny, wide)
+
     for c in (0, 3, 5, 1, 2):
         cx_up[c].wait_recv()
         cx_down[c].wait_recv()
@@ -387,17 +394,10 @@
             osend[k * tall + c * nm : k * tall + (c + 1) * nm, :] = res[
                 k * nm : (k + 1) * nm, c * 2 * ny : (c + 1) * 2 * ny
             ]
-    exchange_start(osend, orecv, o2a_send, o2a_recv, own_sem.at[1])
-
-    for first, wide in pieces:
-        at = slice(first, first + wide)
-        fine = jnp.dot(lhs[0 : 6 * ny, :], tbv[:, at], preferred_element_type=f32)
-        velx[:, 1:3, body, at] = fine.reshape(3, 2, ny, wide)
-        fine = jnp.dot(lhs[0 : 6 * ny, :], tsv[:, at], preferred_element_type=f32)
-        veldz[:, :, :, at] = fine.reshape(3, 2, ny, wide)
 
     vx_up.wait_recv()
     vx_down.wait_recv()
+    exchange_start(osend, orecv, o2a_send, o2a_recv, own_sem.at[1])
 
     @pl.when(has_low)
     def _():

time: 82.4 us -> 81.6 us (level)
    pallas_call x1, Pallas kernels: 78.5 us -> 77.7 us  [shards(): pl.pallas_call(functools.partial(kernel, (ngy, ngz, nm, ny, nz, depth)),...]
where the time goes in v3:
time: 81.6 us; the launch traced here: 81.3 us
  Pallas kernels  77.7 us (95%)
  local copies, waits for them, and re-layouts  3 us (4%)
    pallas_call x1, Pallas kernels, shards(): pl.pallas_call(functools.partial(kernel, (ngy, ngz, nm, ny, nz, depth)),...  77.7 us
    unnamed x2, local copies, waits for them, and re-layouts  3 us

profile of v3, /device:TPU:32, one launch (start us, length us, event | category | flops | bytes accessed | tf_op | source)
XLA Modules:
  0.0 81.3 jit_solution(5764347839498594394)
XLA Ops:
  0.6 77.7 %fene_step.1 = (f32[6,2,64,1152]{3,2,1,0:T(8,128)S(1)}, f32[3456,64]{1,0:T(8,128)S(1)}) custom-call(f32[54,64,64]{2,1,0:T(8,128)} %bitcast.7, f32[6,2,64,1152]{3,2,1,0:T(8,128)} %conf.1, bf16[1280,1152]{1,0:T(8,128)(2,1)} %constant.4.clone.tab_b, bf16[1280,1152]{1,0:T(8,128)(2,1)} %constant.5.clone.tab_s), custom_call_target="tpu_custom_call" | custom-call | tf_op jit(solution)/shard_map/fene_step/pallas_call | solution.py:520
  78.3 1.8 %copy.8 = f32[6,2,64,1152]{3,2,1,0:T(8,128)} copy(f32[6,2,64,1152]{3,2,1,0:T(8,128)S(1)} %get-tuple-element.6) | data formatting | bytes 7077888
  80.1 1.2 %copy.9 = f32[3,64,64,18]{2,1,3,0:T(8,128)} copy(f32[3,64,64,18]{2,1,3,0:T(8,128)S(1)} %bitcast.6) | data formatting | bytes 1769472

commit v4 on v3

--- a/solution.py
+++ b/solution.py
@@ -302,18 +302,26 @@
             cols[c, pl.ds(k * nm, nm), :] = recv[k, c * nm : (c + 1) * nm, :]
 
     exchange_recv(send, recv, a2a_send, a2a_recv, own_sem.at[0], place)
+    vx_up = [
+        pltpu.make_async_remote_copy(
+            rows.at[c, 1], vhalo.at[0, c], vx_send.at[0, c], vx_recv.at[0, c],
+            device_id=(gy, right), device_id_type=MESH,
+        )
+        for c in range(3)
+    ]
+    vx_down = [
+        pltpu.make_async_remote_copy(
+            rows.at[c, 0], vhalo.at[1, c], vx_send.at[1, c], vx_recv.at[1, c],
+            device_id=(gy, left), device_id_type=MESH,
+        )
+        for c in range(3)
+    ]
     for c in range(3):
         turned = cols[c].T
         rows[c] = turned.reshape(2, ny, depth)
-
-    vx_up = pltpu.make_async_remote_copy(
-        rows.at[:, 1], vhalo.at[0], vx_send.at[0], vx_recv.at[0],
-        device_id=(gy, right), device_id_type=MESH,
-    )
-    vx_down = pltpu.make_async_remote_copy(
-        rows.at[:, 0], vhalo.at[1], vx_send.at[1], vx_recv.at[1],
-        device_id=(gy, left), device_id_type=MESH,
-    )
+        vx_up[c].start()
+        vx_down[c].start()
+
     vy_up = pltpu.make_async_remote_copy(
         vedge.at[1], yhalo.at[0], vy_send.at[0], vy_recv.at[0],
         device_id=(gy + 1, gz), device_id_type=MESH,
@@ -322,8 +330,6 @@
         vedge.at[0], yhalo.at[1], vy_send.at[1], vy_recv.at[1],
         device_id=(gy - 1, gz), device_id_type=MESH,
     )
-    vx_up.start()
-    vx_down.start()
     cx_up[4].start()
     cx_down[4].start()
 
@@ -395,8 +401,9 @@
                 k * nm : (k + 1) * nm, c * 2 * ny : (c + 1) * 2 * ny
             ]
 
-    vx_up.wait_recv()
-    vx_down.wait_recv()
+    for c in range(3):
+        vx_up[c].wait_recv()
+        vx_down[c].wait_recv()
     exchange_start(osend, orecv, o2a_send, o2a_recv, own_sem.at[1])
 
     @pl.when(has_low)
@@ -491,8 +498,9 @@
     for c in range(6):
         cx_up[c].wait_send()
         cx_down[c].wait_send()
-    vx_up.wait_send()
-    vx_down.wait_send()
+    for c in range(3):
+        vx_up[c].wait_send()
+        vx_down[c].wait_send()
 
     @pl.when(has_high)
     def _():
@@ -551,7 +559,7 @@
             dma((2,)), dma((4,)), dma((2,)),
             dma((ngz,)), dma((ngz,)), dma((ngz,)), dma((ngz,)),
             dma((2, 6)), dma((2, 6)), dma((2,)), dma((2,)),
-            dma((2,)), dma((2,)), dma((2,)), dma((2,)),
+            dma((2, 3)), dma((2, 3)), dma((2,)), dma((2,)),
         ],
         compiler_params=pltpu.CompilerParams(
             collective_id=0, has_side_effects=True, vmem_limit_bytes=52 << 20

time: 81.6 us -> 81.6 us (level)
  no operation moved by 1% of the time
where the time goes in v4:
time: 81.6 us; the launch traced here: 81.4 us
  Pallas kernels  77.7 us (95%)
  local copies, waits for them, and re-layouts  3 us (4%)
    pallas_call x1, Pallas kernels, shards(): pl.pallas_call(functools.partial(kernel, (ngy, ngz, nm, ny, nz, depth)),...  77.7 us
    unnamed x2, local copies, waits for them, and re-layouts  3 us

profile of v4, /device:TPU:32, one launch (start us, length us, event | category | flops | bytes accessed | tf_op | source)
XLA Modules:
  0.0 81.4 jit_solution(16897934500683041021)
XLA Ops:
  0.6 77.7 %fene_step.1 = (f32[6,2,64,1152]{3,2,1,0:T(8,128)S(1)}, f32[3456,64]{1,0:T(8,128)S(1)}) custom-call(f32[54,64,64]{2,1,0:T(8,128)} %bitcast.7, f32[6,2,64,1152]{3,2,1,0:T(8,128)} %conf.1, bf16[1280,1152]{1,0:T(8,128)(2,1)} %constant.4.clone.tab_b, bf16[1280,1152]{1,0:T(8,128)(2,1)} %constant.5.clone.tab_s), custom_call_target="tpu_custom_call" | custom-call | tf_op jit(solution)/shard_map/fene_step/pallas_call | solution.py:528
  78.4 1.8 %copy.8 = f32[6,2,64,1152]{3,2,1,0:T(8,128)} copy(f32[6,2,64,1152]{3,2,1,0:T(8,128)S(1)} %get-tuple-element.6) | data formatting | bytes 7077888
  80.2 1.2 %copy.9 = f32[3,64,64,18]{2,1,3,0:T(8,128)} copy(f32[3,64,64,18]{2,1,3,0:T(8,128)S(1)} %bitcast.6) | data formatting | bytes 1769472
